TPU v7x, 512 devices: a whole 4x8x8 slice. The times are simulated.
512 devices in a mesh: gx: 16 (over z, core), gy: 32 (over x, y).
Axes of the slice: x: 4, y: 8, z: 8, core: 2. Of those that a mesh axis runs over, the one named last changes fastest.
Arguments:
- control: float32 [16, 4096, 2048], P(None, 'gy', 'gx'), may hold values from -6 to 6
- scale_x: float32 [16, 2048], replicated, may hold values from 2 to 384
- scale_y: float32 [16, 4096], P(None, 'gy'), may hold values from 2 to 384
- vertical_taps: float32 [5, 16], replicated, may hold values from 0.1 to 0.5
Outputs:
- increment: float32 [16, 4096, 2048], P(None, 'gy', 'gx')
All inputs are finite; a program needn't handle non-finite values.
Results may differ from a plain program's by a relative error of at most 0.00016.
Values sent between devices are 32-bit elements; how exact they have to be, the bound alone decides.
No kernel may reach another device: no remote copies, remote signals or barrier semaphores. Data moves between devices by JAX's collectives and lax.ppermute only.
A program may use at most 64 MiB of HBM per device.

v0:
```python
import functools
import jax
import jax.numpy as jnp
from jax import lax
from jax.experimental import pallas as pl
from jax.experimental.pallas import tpu as pltpu
from jax.sharding import PartitionSpec as P


F32 = jnp.float32
BF16 = jnp.bfloat16
N = 128
HALF = 64
GRANT = 16 << 20


def split(a):
    high = a.astype(BF16)
    return high, (a - high.astype(F32)).astype(BF16)


def dot3(a, b, dims):
    ah, al = a if isinstance(a, tuple) else split(a)
    bh, bl = b if isinstance(b, tuple) else split(b)

    def one(u, v):
        return lax.dot_general(u, v, (dims, ((), ())), preferred_element_type=F32)

    return one(ah, bh) + (one(ah, bl) + one(al, bh))


NN = ((1,), (0,))
NT = ((1,), (1,))
TN = ((0,), (0,))


def poly(a, b):
    out = []
    for k in range(4):
        total = a[0] * b[k]
        for m in range(1, k + 1):
            total = total + a[m] * b[k - m]
        out.append(total)
    return out


def geometric(lead, q):
    out = [lead]
    for _ in range(3):
        out.append(out[-1] * q)
    return out


def sym(table, a, b):
    return table[(max(a, b), min(a, b))]


def congruence(t, r):
    x = {}
    for c in range(4):
        for a in range(4):
            total = t[0] * sym(r, a, c)
            for m in range(1, a + 1):
                total = total + t[m] * sym(r, a - m, c)
            x[(a, c)] = total
    out = {}
    for a in range(4):
        for b in range(a + 1):
            total = t[0] * x[(a, b)]
            for m in range(1, b + 1):
                total = total + t[m] * x[(a, b - m)]
            out[(a, b)] = total
    return out


def lanes(shape):
    return lax.broadcasted_iota(jnp.int32, shape, len(shape) - 1)


def later(x, d, fill):
    moved = pltpu.roll(x, N - d, 1)
    return jnp.where(lanes(x.shape) < N - d, moved, fill)


def earlier(x, d, fill):
    moved = pltpu.roll(x, d, 1)
    return jnp.where(lanes(x.shape) >= d, moved, fill)


def ones_first(k):
    return 1.0 if k == 0 else 0.0


def poles(scale):
    p = jnp.exp(-1.0 / scale)
    return p, 1.0 - p


def suffix_scan(p, q):
    t = geometric(p, q)
    g = [p * q]
    for _ in range(6):
        g.append(g[-1] * q)
    r = {(a, b): g[a + b] for a in range(4) for b in range(a + 1)}
    d = 1
    while d < N:
        t2 = [later(t[k], d, ones_first(k)) for k in range(4)]
        r2 = {key: later(value, d, 0.0) for key, value in r.items()}
        grown = congruence(t, r2)
        r = {key: r[key] + grown[key] for key in r}
        t = poly(t, t2)
        d *= 2
    return t, r


def prefix_scan(p, q):
    t = geometric(p, q)
    d = 1
    while d < N:
        t = poly(t, [earlier(t[k], d, ones_first(k)) for k in range(4)])
        d *= 2
    return t


def return_map(r, s):
    out = []
    for a in range(4):
        total = sym(r, a, 3) * s[0]
        for b in range(1, 4):
            total = total + sym(r, a, 3 - b) * s[b]
        out.append(total)
    return out


def extraction(p, q, t, r, before):
    inject = geometric(q, q)
    t_next = [later(t[k], 1, ones_first(k)) for k in range(4)]
    r_next = {key: later(value, 1, 0.0) for key, value in r.items()}
    f = poly(t_next, inject)
    back = poly(geometric(p, q), return_map(r_next, inject))
    back = [back[k] + inject[k] * inject[3] for k in range(4)]
    px = [earlier(before[k], 1, ones_first(k)) for k in range(4)]
    return f, poly(px, back)


def response(t, r, before):
    px = [earlier(before[k], 1, ones_first(k)) for k in range(4)]
    out = []
    for k in range(4):
        total = sym(r, 3, 3 - k) * px[0]
        for b in range(k + 1, 4):
            total = total + sym(r, 3, 3 - b) * px[b - k]
        out.append(total)
    return out + [t[3 - k] for k in range(4)]


COEFS = [(a, b) for a in range(4) for b in range(a + 1)]


def own_scale(axis, scale_ref):
    if axis is None:
        return scale_ref[...]
    me = lax.axis_index(axis)
    return scale_ref[:, pl.ds(pl.multiple_of(me * N, N), N)]


def states_x_kernel(scale_ref, control_ref, out_ref, weights):
    scale = own_scale("gx", scale_ref)
    p, q = poles(scale)
    t, r = suffix_scan(p, q)
    before = prefix_scan(p, q)
    f, b = extraction(p, q, t, r, before)
    amplitude = jnp.sqrt(8.0 * scale)
    for k in range(4):
        weights[:, k, :] = f[k] * amplitude
        weights[:, 4 + k, :] = b[k] * amplitude
    for level in range(out_ref.shape[0]):
        out_ref[level] = dot3(weights[level], control_ref[level], NT)


def link_x_kernel(scale_ref, out_ref, gathered, spread):
    blocks = out_ref.shape[0] // 8
    me = lax.axis_index("gx")
    level = lax.broadcasted_iota(jnp.int32, (scale_ref.shape[0], N), 0)
    for j in range(blocks):
        block = jnp.where(level == me, scale_ref[:, j * N:(j + 1) * N], 0.0)
        gathered[j:j + 1, :] = jnp.sum(block, axis=0, keepdims=True)
    p, q = poles(gathered[...])
    t, r = suffix_scan(p, q)
    for k in range(4):
        spread[k] = jnp.broadcast_to(t[k][:, 0:1], (blocks, N))
    for m, key in enumerate(COEFS):
        spread[4 + m] = jnp.broadcast_to(r[key][:, 0:1], (blocks, N))
    lane = lanes((1, N))
    run_links(
        blocks,
        lambda j, k: (lane == 8 * j + k).astype(F32),
        spread,
        lambda j, k, value: out_ref.__setitem__((pl.ds(8 * j + k, 1), slice(None)), value),
    )


def run_links(blocks, source, spread, store):
    zero = jnp.zeros((1, N), F32)
    s = [zero] * 4
    returns = []
    for j in range(blocks):
        t = [spread[k, j:j + 1, :] for k in range(4)]
        r = {key: spread[4 + m, j:j + 1, :] for m, key in enumerate(COEFS)}
        for k in range(4):
            store(j, k, s[k])
        back = return_map(r, s)
        returns.append([back[k] + source(j, 4 + k) for k in range(4)])
        moved = poly(t, s)
        s = [moved[k] + source(j, k) for k in range(4)]
    e = [zero] * 4
    for j in reversed(range(blocks)):
        t = [spread[k, j:j + 1, :] for k in range(4)]
        for k in range(4):
            store(j, 4 + k, e[k])
        moved = poly(t, e)
        e = [moved[k] + returns[j][k] for k in range(4)]


def apply_x_kernel(link_ref, states_ref, out_ref):
    blocks = out_ref.shape[0]
    flat = states_ref[...].reshape(blocks * 8, N)
    out_ref[...] = dot3(link_ref[...], flat, NN).reshape(blocks, 8, N)


def filter_kernel(axis, scale_ref, local_ref, spread, middle):
    scale = own_scale(axis, scale_ref)
    levels = scale.shape[0]
    p, q = poles(scale)
    for i in range(N):
        spread[i] = jnp.broadcast_to(p[:, i:i + 1], (levels, N))
    shape = (levels, N)
    lane = lanes(shape)
    zero = jnp.zeros(shape, F32)
    column = jnp.sqrt(8.0 * scale) if axis is None else p / q

    def advance(factor, state, inflow):
        rest = 1.0 - factor
        out = []
        for k in range(4):
            inflow = factor * state[k] + rest * inflow
            out.append(inflow)
        return out

    def forward(i, state):
        state = advance(spread[i], state, (lane == i).astype(F32))
        middle[i] = state[3]
        return tuple(state)

    lax.fori_loop(0, N, forward, (zero,) * 4, unroll=8)

    def backward(k, state):
        i = N - 1 - k
        state = advance(spread[i], state, middle[i])
        local_ref[:, pl.ds(i, 1), :] = (state[3] * column).reshape(levels, 1, N)
        return tuple(state)

    lax.fori_loop(0, N, backward, (zero,) * 4, unroll=8)


def tables_kernel(scale_x_ref, scale_y_ref, entry_x_ref, gain_x_ref, extract_ref, entry_y_ref, coef_ref):
    levels = scale_y_ref.shape[0]
    scale = jnp.concatenate([own_scale("gx", scale_x_ref), scale_y_ref[...]], 0)
    p, q = poles(scale)
    t, r = suffix_scan(p, q)
    before = prefix_scan(p, q)
    amplitude = jnp.sqrt(8.0 * scale)
    gain_x_ref[...] = (amplitude * q / p)[:levels]
    for k, row in enumerate(response(t, r, before)):
        entry_x_ref[:, k, :] = row[:levels]
        entry_y_ref[:, k, :] = row[levels:]
    p, q, amplitude = p[levels:], q[levels:], amplitude[levels:]
    t = [value[levels:] for value in t]
    r = {key: value[levels:] for key, value in r.items()}
    f, b = extraction(p, q, t, r, [value[levels:] for value in before])
    for k in range(4):
        extract_ref[:, k, :] = f[k] * amplitude
        extract_ref[:, 4 + k, :] = b[k] * amplitude
    shape = p.shape
    lane = lanes(shape)
    coefs = jnp.zeros(shape, F32)
    for m, value in enumerate(t + [r[key] for key in COEFS]):
        coefs = jnp.where(lane == HALF + m, jnp.broadcast_to(value[:, 0:1], shape), coefs)
    coef_ref[...] = coefs


def local_x_kernel(control_ref, gain_ref, filter_ref, extract_ref, out_ref, base_ref):
    for level in range(out_ref.shape[0]):
        g = dot3(control_ref[level] * gain_ref[level:level + 1, :], filter_ref[level], NN)
        out_ref[level] = g
        base_ref[level] = dot3(extract_ref[level], g, NN)


def states_y_kernel(enter_ref, entry_ref, extract_ref, base_ref, coef_ref, out_ref):
    left = lanes((8, N)) < HALF
    for level in range(base_ref.shape[0]):
        corner = dot3(extract_ref[level], enter_ref[level], NT)
        states = base_ref[level] + dot3(corner, entry_ref[level], NN)
        coefs = jnp.broadcast_to(coef_ref[level:level + 1, :], (8, N))
        out_ref[2 * level] = jnp.where(left, states, coefs)
        out_ref[2 * level + 1] = jnp.where(left, pltpu.roll(states, HALF, 1), coefs)


def apply_y_kernel(states_ref, out_ref, spread, links):
    blocks = states_ref.shape[0]
    coefs = states_ref[:, 0, :]
    for m in range(4 + len(COEFS)):
        spread[m] = jnp.broadcast_to(coefs[:, HALF + m:HALF + m + 1], (blocks, N))
    run_links(
        blocks,
        lambda j, k: states_ref[j, k:k + 1, :],
        spread,
        lambda j, k, value: links.__setitem__((j, slice(k, k + 1), slice(None)), value),
    )
    left = lanes((4, N)) < HALF
    for j in range(blocks):
        out_ref[j] = jnp.where(left, links[j, 0:4, :], pltpu.roll(links[j, 4:8, :], HALF, 1))


def local_y_kernel(base_ref, enter_ref, entry_ref, filter_ref, out_ref):
    for level in range(out_ref.shape[0]):
        rows = base_ref[level] + dot3(enter_ref[level], entry_ref[level], TN)
        out_ref[level] = dot3(filter_ref[level], rows, NN)


def vertical_kernel(taps_ref, values_ref, out_ref):
    levels = out_ref.shape[0]
    for level in range(levels):
        total = None
        for d in range(5):
            other = level + d - 2
            if 0 <= other < levels:
                term = taps_ref[d, level] * values_ref[other]
                total = term if total is None else total + term
        out_ref[level] = total


def final_kernel(taps_ref, values_ref, slots_ref, entry_ref, out_ref, enter):
    levels = out_ref.shape[0]
    left = lanes((4, N)) < HALF
    for level in range(levels):
        a, b = slots_ref[2 * level], slots_ref[2 * level + 1]
        enter[level, 0:4, :] = jnp.where(left, a, pltpu.roll(b, HALF, 1))
        enter[level, 4:8, :] = jnp.where(left, pltpu.roll(a, HALF, 1), b)
    for level in range(levels):
        weights, states = [], []
        for d in range(5):
            other = level + d - 2
            if 0 <= other < levels:
                weights.append(taps_ref[d, level] * entry_ref[other])
                states.append(enter[other])
        weights = jnp.concatenate(weights, 0)
        states = jnp.concatenate(states, 0)
        out_ref[level] = values_ref[level] + dot3(weights, states, TN)


VM = pl.BlockSpec(memory_space=pltpu.VMEM)
SM = pl.BlockSpec(memory_space=pltpu.SMEM)


def call(kernel, shapes, args, scratch=(), flops=0, smem=()):
    outs = [jax.ShapeDtypeStruct(shape, F32) for shape in shapes]
    moved = 4 * sum(x.size for x in list(args) + outs)
    result = pl.pallas_call(
        kernel,
        out_shape=outs if len(outs) > 1 else outs[0],
        in_specs=[SM if k in smem else VM for k in range(len(args))],
        out_specs=[VM] * len(outs) if len(outs) > 1 else VM,
        scratch_shapes=[pltpu.VMEM(shape, F32) for shape in scratch],
        compiler_params=pltpu.CompilerParams(vmem_limit_bytes=GRANT),
        cost_estimate=pl.CostEstimate(flops=flops, bytes_accessed=moved, transcendentals=0),
    )(*args)
    return result


def exchange(value, axis):
    return lax.all_to_all(value, axis, 0, 0, tiled=True)


def steps(control, scale_x, scale_y, taps):
    levels = control.shape[0]
    full, small = (levels, N, N), (levels, 8, N)
    nx, ny = lax.axis_size("gx"), lax.axis_size("gy")
    table = (N, levels, N)
    bind = functools.partial

    closing = call(states_x_kernel, [small], (scale_x, control), [small])
    closing = exchange(closing, "gx")
    link = call(link_x_kernel, [(8 * nx, N)], (scale_x,), [(nx, N), (14, nx, N)])
    filter_x = call(bind(filter_kernel, "gx"), [full], (scale_x,), [table, table])

    enter_x = call(apply_x_kernel, [small], (link, closing))
    enter_x = exchange(enter_x, "gx")
    entry_x, gain_x, extract_y, entry_y, coefs = call(
        tables_kernel, [small, (levels, N), small, small, (levels, N)], (scale_x, scale_y)
    )
    local, base = call(local_x_kernel, [full, small], (control, gain_x, filter_x, extract_y))

    slots = call(states_y_kernel, [(ny, 8, N)], (enter_x, entry_x, extract_y, base, coefs))
    slots = exchange(slots, "gy")
    filter_y = call(bind(filter_kernel, None), [full], (scale_y,), [table, table])
    local = call(local_y_kernel, [full], (local, enter_x, entry_x, filter_y))

    slots = call(apply_y_kernel, [(ny, 4, N)], (slots,), [(14, ny, N), (ny, 8, N)])
    slots = exchange(slots, "gy")
    local = call(vertical_kernel, [full], (taps, local), smem=(0,))
    return call(final_kernel, [full], (taps, local, slots, entry_y), [small], smem=(0,))


def solution(mesh):
    return jax.shard_map(
        steps,
        mesh=mesh,
        in_specs=(P(None, "gy", "gx"), P(), P(None, "gy"), P()),
        out_specs=P(None, "gy", "gx"),
        check_vma=False,
    )
```

profile of v0, /device:TPU:1, one launch (start us, length us, event | category | flops | bytes accessed | tf_op | source)
XLA Modules:
  0.0 72.8 jit_solution(9854879541693179027)
XLA Ops:
  0.0 1.2 %copy-done = f32[16,128,128]{2,1,0:T(8,128)S(1)} copy-done((f32[16,128,128]{2,1,0:T(8,128)S(1)}, f32[16,128,128]{2,1,0:T(8,128)}, u32[]{:S(2)}) %copy-start) | copy-done | bytes 1048600
  1.2 0.9 %copy-done.2 = f32[16,2048]{1,0:T(8,128)S(1)} copy-done((f32[16,2048]{1,0:T(8,128)S(1)}, f32[16,2048]{1,0:T(8,128)}, u32[]{:S(2)}) %copy-start.2) | copy-done | bytes 131096
  2.1 2.5 %shard_map.50 = f32[16,8,128]{2,1,0:T(8,128)} custom-call(f32[16,2048]{1,0:T(8,128)S(1)} %copy-done.2, f32[16,128,128]{2,1,0:T(8,128)S(1)} %copy-done), custom_call_target="tpu_custom_call" | custom-call | bytes 1245184 | tf_op jit(solution)/shard_map/pallas_call | solution.py:369
  4.6 12.0 %all-to-all-start = ((f32[16,8,128]{2,1,0:T(8,128)}), f32[16,8,128]{2,1,0:T(8,128)S(1)}, u32[]{:S(2)}, u32[]{:S(2)}) async-start(f32[16,8,128]{2,1,0:T(8,128)} %shard_map.50), calls=%async_computation | async-start | bytes 131072 | tf_op jit(solution)/shard_map/all_to_all | solution.py:382
  16.6 1.0 %shard_map.49.link_ref = f32[128,128]{1,0:T(8,128)S(1)} custom-call(f32[16,2048]{1,0:T(8,128)S(1)} %copy-done.3), custom_call_target="tpu_custom_call" | custom-call | bytes 196608 | tf_op jit(solution)/shard_map/pallas_call | solution.py:369
  17.6 6.8 %all-to-all-done.states_ref = f32[16,8,128]{2,1,0:T(8,128)S(1)} async-done(((f32[16,8,128]{2,1,0:T(8,128)}), f32[16,8,128]{2,1,0:T(8,128)S(1)}, u32[]{:S(2)}, u32[]{:S(2)}) %all-to-all-start) | async-done | bytes 65568 | tf_op jit(solution)/shard_map/all_to_all | solution.py:382
  24.4 0.8 %shard_map.51 = f32[16,8,128]{2,1,0:T(8,128)} custom-call(f32[128,128]{1,0:T(8,128)S(1)} %shard_map.49.link_ref, f32[16,8,128]{2,1,0:T(8,128)S(1)} %all-to-all-done.states_ref), custom_call_target="tpu_custom_call" | custom-call | bytes 196608 | tf_op jit(solution)/shard_map/pallas_call | solution.py:369
  25.2 3.4 %all-to-all-start.1 = ((f32[16,8,128]{2,1,0:T(8,128)}), f32[16,8,128]{2,1,0:T(8,128)S(1)}, u32[]{:S(2)}, u32[]{:S(2)}) async-start(f32[16,8,128]{2,1,0:T(8,128)} %shard_map.51), calls=%async_computation.1 | async-start | bytes 131072 | tf_op jit(solution)/shard_map/all_to_all | solution.py:382
  28.6 0.0 copy-start.4
  28.6 2.9 %shard_map.47.filter_ref = f32[16,128,128]{2,1,0:T(8,128)S(1)} custom-call(f32[16,2048]{1,0:T(8,128)S(1)} %copy-done.3), custom_call_target="tpu_custom_call" | custom-call | bytes 1179648 | tf_op jit(solution)/shard_map/pallas_call | solution.py:369
  31.5 1.0 %shard_map.46 = (f32[16,8,128]{2,1,0:T(8,128)S(1)}, f32[16,128]{1,0:T(8,128)S(1)}, f32[16,8,128]{2,1,0:T(8,128)S(1)}, f32[16,8,128]{2,1,0:T(8,128)S(1)}, f32[16,128]{1,0:T(8,128)S(1)}) custom-call(f32[16,2048]{1,0:T(8,128)S(1)} %copy-done.3, f32[16,128]{1,0:T(8,128)S(1)} %copy-done.4), custom_call_target="tpu_custom_call" | custom-call | bytes 352256 | tf_op jit(solution)/shard_map/pallas_call | solution.py:369
  32.5 1.1 %shard_map.48 = (f32[16,128,128]{2,1,0:T(8,128)S(1)}, f32[16,8,128]{2,1,0:T(8,128)S(1)}) custom-call(f32[16,128,128]{2,1,0:T(8,128)S(1)} %copy-done.1, f32[16,128]{1,0:T(8,128)S(1)} %get-tuple-element.12.gain_ref, f32[16,128,128]{2,1,0:T(8,128)S(1)} %shard_map.47.filter_ref, f32[16,8,128]{2,1,0:T(8,128)S(1)} %get-tuple-element.13.extract_ref), custom_call_target="tpu_custom_call" | custom-call | bytes 3284992 | tf_op jit(solution)/shard_map/pallas_call | solution.py:369
  33.6 2.7 %all-to-all-done.1.enter_ref = f32[16,8,128]{2,1,0:T(8,128)S(1)} async-done(((f32[16,8,128]{2,1,0:T(8,128)}), f32[16,8,128]{2,1,0:T(8,128)S(1)}, u32[]{:S(2)}, u32[]{:S(2)}) %all-to-all-start.1) | async-done | bytes 65568 | tf_op jit(solution)/shard_map/all_to_all | solution.py:382
  36.4 0.7 shard_map.55
  37.1 18.6 %all_to_all.20.states_ref = f32[32,8,128]{2,1,0:T(8,128)S(1)} all-to-all(f32[32,8,128]{2,1,0:T(8,128)S(1)} %shard_map.55), channel_id=1, replica_groups=mesh['gx'=16,'gy'=32] {'gy'}, dimensions={0} | all-to-all | bytes 262144 | tf_op jit(solution)/shard_map/all_to_all | solution.py:382
  55.7 1.5 %shard_map.56 = f32[32,4,128]{2,1,0:T(4,128)} custom-call(f32[32,8,128]{2,1,0:T(8,128)S(1)} %all_to_all.20.states_ref), custom_call_target="tpu_custom_call" | custom-call | bytes 196608 | tf_op jit(solution)/shard_map/pallas_call | solution.py:369
  57.2 4.4 %all-to-all-start.3 = ((f32[32,4,128]{2,1,0:T(4,128)}), f32[32,4,128]{2,1,0:T(4,128)S(1)}, u32[]{:S(2)}, u32[]{:S(2)}) async-start(f32[32,4,128]{2,1,0:T(4,128)} %shard_map.56), calls=%async_computation.3 | async-start | bytes 131072 | tf_op jit(solution)/shard_map/all_to_all | solution.py:382
  61.6 2.9 %shard_map.52.filter_ref = f32[16,128,128]{2,1,0:T(8,128)S(1)} custom-call(f32[16,128]{1,0:T(8,128)S(1)} %copy-done.4), custom_call_target="tpu_custom_call" | custom-call | bytes 1056768 | tf_op jit(solution)/shard_map/pallas_call | solution.py:369
  64.5 0.0 copy-start.5
  64.5 1.2 %shard_map.53.values_ref = f32[16,128,128]{2,1,0:T(8,128)S(1)} custom-call(f32[16,128,128]{2,1,0:T(8,128)S(1)} %get-tuple-element.14.base_ref, f32[16,8,128]{2,1,0:T(8,128)S(1)} %all-to-all-done.1.enter_ref, f32[16,8,128]{2,1,0:T(8,128)S(1)} %get-tuple-element.15.entry_ref, f32[16,128,128]{2,1,0:T(8,128)S(1)} %shard_map.52.filter_ref), custom_call_target="tpu_custom_call" | custom-call | bytes 3276800 | tf_op jit(solution)/shard_map/pallas_call | solution.py:369
  65.7 0.0 copy-done.5
  65.7 0.9 %shard_map.54.values_ref = f32[16,128,128]{2,1,0:T(8,128)S(1)} custom-call(f32[5,16]{1,0:T(8,128)S(1)} %copy-done.5, f32[16,128,128]{2,1,0:T(8,128)S(1)} %shard_map.53.values_ref), custom_call_target="tpu_custom_call" | custom-call | bytes 2097472 | tf_op jit(solution)/shard_map/pallas_call | solution.py:369
  66.6 4.0 %all-to-all-done.3.slots_ref = f32[32,4,128]{2,1,0:T(4,128)S(1)} async-done(((f32[32,4,128]{2,1,0:T(4,128)}), f32[32,4,128]{2,1,0:T(4,128)S(1)}, u32[]{:S(2)}, u32[]{:S(2)}) %all-to-all-start.3) | async-done | bytes 65568 | tf_op jit(solution)/shard_map/all_to_all | solution.py:382
  70.6 2.2 %shard_map.57 = f32[16,128,128]{2,1,0:T(8,128)} custom-call(f32[5,16]{1,0:T(8,128)S(1)} %copy-done.5, f32[16,128,128]{2,1,0:T(8,128)S(1)} %shard_map.54.values_ref, f32[32,4,128]{2,1,0:T(4,128)S(1)} %all-to-all-done.3.slots_ref, f32[16,8,128]{2,1,0:T(8,128)S(1)} %get-tuple-element.18.entry_ref), custom_call_target="tpu_custom_call" | custom-call | bytes 2228544 | tf_op jit(solution)/shard_map/pallas_call | solution.py:369
  (7 shorter events, 0.0 us)
Async XLA Ops:
  0.0 1.2 %copy-start = (f32[16,128,128]{2,1,0:T(8,128)S(1)}, f32[16,128,128]{2,1,0:T(8,128)}, u32[]{:S(2)}) copy-start(f32[16,128,128]{2,1,0:T(8,128)} %control_ref.3) | copy-start | bytes 3145732
  1.2 0.9 %copy-start.2 = (f32[16,2048]{1,0:T(8,128)S(1)}, f32[16,2048]{1,0:T(8,128)}, u32[]{:S(2)}) copy-start(f32[16,2048]{1,0:T(8,128)} %scale_ref.6) | copy-start | bytes 393220
  2.1 14.5 %copy-start.3 = (f32[16,2048]{1,0:T(8,128)S(1)}, f32[16,2048]{1,0:T(8,128)}, u32[]{:S(2)}) copy-start(f32[16,2048]{1,0:T(8,128)} %scale_ref.6) | copy-start | bytes 393220
  4.6 27.9 %copy-start.1 = (f32[16,128,128]{2,1,0:T(8,128)S(1)}, f32[16,128,128]{2,1,0:T(8,128)}, u32[]{:S(2)}) copy-start(f32[16,128,128]{2,1,0:T(8,128)} %control_ref.3) | copy-start | bytes 3145732
  4.6 19.7 %all-to-all-start = ((f32[16,8,128]{2,1,0:T(8,128)}), f32[16,8,128]{2,1,0:T(8,128)S(1)}, u32[]{:S(2)}, u32[]{:S(2)}) async-start(f32[16,8,128]{2,1,0:T(8,128)} %shard_map.50), calls=%async_computation | async-start | bytes 131072 | tf_op jit(solution)/shard_map/all_to_all | solution.py:382
  25.2 11.2 %all-to-all-start.1 = ((f32[16,8,128]{2,1,0:T(8,128)}), f32[16,8,128]{2,1,0:T(8,128)S(1)}, u32[]{:S(2)}, u32[]{:S(2)}) async-start(f32[16,8,128]{2,1,0:T(8,128)} %shard_map.51), calls=%async_computation.1 | async-start | bytes 131072 | tf_op jit(solution)/shard_map/all_to_all | solution.py:382
  28.6 2.9 %copy-start.4 = (f32[16,128]{1,0:T(8,128)S(1)}, f32[16,128]{1,0:T(8,128)}, u32[]{:S(2)}) copy-start(f32[16,128]{1,0:T(8,128)} %scale_ref.7) | copy-start | bytes 24580
  57.2 13.4 %all-to-all-start.3 = ((f32[32,4,128]{2,1,0:T(4,128)}), f32[32,4,128]{2,1,0:T(4,128)S(1)}, u32[]{:S(2)}, u32[]{:S(2)}) async-start(f32[32,4,128]{2,1,0:T(4,128)} %shard_map.56), calls=%async_computation.3 | async-start | bytes 131072 | tf_op jit(solution)/shard_map/all_to_all | solution.py:382
  64.5 1.2 %copy-start.5 = (f32[5,16]{1,0:T(8,128)S(1)}, f32[5,16]{1,0:T(8,128)}, u32[]{:S(2)}) copy-start(f32[5,16]{1,0:T(8,128)} %taps_ref.3) | copy-start | bytes 964
where the time goes:
time: 73.6 us; the launch traced here: 72.8 us
  starting transfers between devices  19.8 us (27%)
  Pallas kernels  18.7 us (25%)
  blocking collectives  18.6 us (25%)
  waiting for transfers between devices  13.5 us (18%)
  local copies, waits for them, and re-layouts  2.15 us (3%)
    all_to_all x3, starting transfers between devices, exchange(): return lax.all_to_all(value, axis, 0, 0, tiled=True)  19.8 us
    pallas_call x12, Pallas kernels, call(): pl.pallas_call(kernel, out_shape=outs if len(outs) > 1 else outs[0], in_s...  18.7 us
    all_to_all x1, blocking collectives, exchange(): return lax.all_to_all(value, axis, 0, 0, tiled=True)  18.6 us
    all_to_all x3, waiting for transfers between devices, exchange(): return lax.all_to_all(value, axis, 0, 0, tiled=True)  13.5 us
    unnamed x12, local copies, waits for them, and re-layouts  2.15 us
  transfers between devices with their start and end apart: 3, of which 3 were waited for; matrix products, arithmetic and copies ran while one was open for 0% of the time, Pallas kernels for 15%

commit v1 on v0

--- a/solution.py
+++ b/solution.py
@@ -12,6 +12,8 @@
 N = 128
 HALF = 64
 GRANT = 16 << 20
+CHUNK = 4
+SENT = 8
 
 
 def split(a):
@@ -27,6 +29,21 @@
         return lax.dot_general(u, v, (dims, ((), ())), preferred_element_type=F32)
 
     return one(ah, bh) + (one(ah, bl) + one(al, bh))
+
+
+def wide_left(a):
+    return jnp.concatenate(split(a), 1)
+
+
+def wide_right(b):
+    high, low = split(b)
+    top = jnp.concatenate([high, low], 1)
+    return jnp.concatenate([top, jnp.concatenate([high, jnp.zeros_like(low)], 1)], 0)
+
+
+def wide_dot(left, right):
+    both = lax.dot_general(left, right, (NN, ((), ())), preferred_element_type=F32)
+    return both[:, :N] + both[:, N:]
 
 
 NN = ((1,), (0,))
@@ -164,18 +181,38 @@
     return scale_ref[:, pl.ds(pl.multiple_of(me * N, N), N)]
 
 
-def states_x_kernel(scale_ref, control_ref, out_ref, weights):
-    scale = own_scale("gx", scale_ref)
+def flat(value):
+    return value.reshape(value.shape[0] * value.shape[1], value.shape[2])
+
+
+def states_x_kernel(scale_hbm, control_hbm, out_ref, scale_ref, control_ref, weights, sems):
+    levels = out_ref.shape[0]
+    me = lax.axis_index("gx")
+    first = pltpu.make_async_copy(
+        scale_hbm.at[:, pl.ds(pl.multiple_of(me * N, N), N)], scale_ref, sems.at[0]
+    )
+    second = pltpu.make_async_copy(control_hbm, control_ref, sems.at[1])
+    first.start()
+    second.start()
+    first.wait()
+    scale = scale_ref[...]
     p, q = poles(scale)
     t, r = suffix_scan(p, q)
     before = prefix_scan(p, q)
     f, b = extraction(p, q, t, r, before)
     amplitude = jnp.sqrt(8.0 * scale)
     for k in range(4):
-        weights[:, k, :] = f[k] * amplitude
-        weights[:, 4 + k, :] = b[k] * amplitude
-    for level in range(out_ref.shape[0]):
-        out_ref[level] = dot3(weights[level], control_ref[level], NT)
+        weights[pl.ds(k, levels, stride=8), :] = f[k] * amplitude
+        weights[pl.ds(4 + k, levels, stride=8), :] = b[k] * amplitude
+    right = wide_right(weights[...].T)
+    owner = lanes((N, N)) // 8
+    total = jnp.zeros((N, N), F32)
+    second.wait()
+    for level in range(0, levels, CHUNK):
+        every = wide_dot(wide_left(flat(control_ref[level:level + CHUNK])), right)
+        for k in range(CHUNK):
+            total = jnp.where(owner == level + k, every[k * N:(k + 1) * N], total)
+    out_ref[...] = total.T.reshape(levels, 8, N)
 
 
 def link_x_kernel(scale_ref, out_ref, gathered, spread):
@@ -297,29 +334,83 @@
 
 
 def states_y_kernel(enter_ref, entry_ref, extract_ref, base_ref, coef_ref, out_ref):
+    levels = base_ref.shape[0]
+    corner = dot3(flat(extract_ref[...]), flat(enter_ref[...]), NT)
+    here = lax.broadcasted_iota(jnp.int32, (N, N), 0) // 8 == lanes((N, N)) // 8
+    corner = jnp.where(here, corner, 0.0)
+    states = flat(base_ref[...]) + dot3(corner, flat(entry_ref[...]), NN)
     left = lanes((8, N)) < HALF
-    for level in range(base_ref.shape[0]):
-        corner = dot3(extract_ref[level], enter_ref[level], NT)
-        states = base_ref[level] + dot3(corner, entry_ref[level], NN)
+    for level in range(levels):
+        own = states[8 * level:8 * level + 8]
         coefs = jnp.broadcast_to(coef_ref[level:level + 1, :], (8, N))
-        out_ref[2 * level] = jnp.where(left, states, coefs)
-        out_ref[2 * level + 1] = jnp.where(left, pltpu.roll(states, HALF, 1), coefs)
-
-
-def apply_y_kernel(states_ref, out_ref, spread, links):
-    blocks = states_ref.shape[0]
-    coefs = states_ref[:, 0, :]
-    for m in range(4 + len(COEFS)):
-        spread[m] = jnp.broadcast_to(coefs[:, HALF + m:HALF + m + 1], (blocks, N))
-    run_links(
-        blocks,
-        lambda j, k: states_ref[j, k:k + 1, :],
-        spread,
-        lambda j, k, value: links.__setitem__((j, slice(k, k + 1), slice(None)), value),
-    )
-    left = lanes((4, N)) < HALF
-    for j in range(blocks):
-        out_ref[j] = jnp.where(left, links[j, 0:4, :], pltpu.roll(links[j, 4:8, :], HALF, 1))
+        out_ref[2 * level] = jnp.where(left, own, coefs)
+        out_ref[2 * level + 1] = jnp.where(left, pltpu.roll(own, HALF, 1), coefs)
+
+
+def run_groups(groups, size, reverse, maps, source, store, ends, starts):
+    steps = range(size - 1, -1, -1) if reverse else range(size)
+    total, state, kept = None, None, []
+    for j in steps:
+        kept.append((j, total, state))
+        t, f = maps(j), source(j)
+        state = f if state is None else [a + b for a, b in zip(poly(t, state), f)]
+        total = t if total is None else poly(t, total)
+    for k in range(4):
+        ends[k], ends[4 + k] = total[k], state[k]
+    enter = [jnp.zeros((1, N), F32)] * 4
+    for c in range(groups - 1, -1, -1) if reverse else range(groups):
+        row = slice(c, c + 1)
+        for k in range(4):
+            starts[k, row, :] = enter[k]
+        moved = poly([ends[k, row, :] for k in range(4)], enter)
+        enter = [moved[k] + ends[4 + k, row, :] for k in range(4)]
+    enter = [starts[k] for k in range(4)]
+    for j, total, state in kept:
+        store(j, enter if total is None else [a + b for a, b in zip(poly(total, enter), state)])
+
+
+def apply_y_kernel(states_ref, out_ref, packed, spread, links, returns, ends, starts):
+    blocks = states_ref.shape[0] // 8
+    groups = ends.shape[1]
+    size = blocks // groups
+    packed[...] = states_ref[pl.ds(0, blocks, stride=8), :]
+
+    def coef(m):
+        return jnp.broadcast_to(packed[:, HALF + m:HALF + m + 1], (blocks, N))
+
+    for m in range(4):
+        spread[m] = coef(m)
+
+    def rows(j):
+        return pl.ds(j, groups, stride=size)
+
+    def store(first):
+        def put(j, values):
+            for k in range(4):
+                links[first + k, rows(j), :] = values[k]
+
+        return put
+
+    def maps(j):
+        return [spread[k, rows(j), :] for k in range(4)]
+
+    for k in range(4):
+        returns[k] = states_ref[pl.ds(k, blocks, stride=8), :]
+
+    def source(j):
+        return [returns[k, rows(j), :] for k in range(4)]
+
+    run_groups(groups, size, False, maps, source, store(0), ends, starts)
+    r = {key: coef(4 + m) for m, key in enumerate(COEFS)}
+    back = return_map(r, [links[k] for k in range(4)])
+    for k in range(4):
+        returns[k] = back[k] + states_ref[pl.ds(4 + k, blocks, stride=8), :]
+    run_groups(groups, size, True, maps, source, store(4), ends, starts)
+    left = lanes((blocks, N)) < HALF
+    for k in range(4):
+        out_ref[pl.ds(k, blocks, stride=4), :] = jnp.where(
+            left, links[k], pltpu.roll(links[4 + k], HALF, 1)
+        )
 
 
 def local_y_kernel(base_ref, enter_ref, entry_ref, filter_ref, out_ref):
@@ -328,54 +419,66 @@
         out_ref[level] = dot3(filter_ref[level], rows, NN)
 
 
-def vertical_kernel(taps_ref, values_ref, out_ref):
+def vertical_kernel(taps_ref, values_ref, entry_ref, out_ref, wide_ref):
     levels = out_ref.shape[0]
+    turned = flat(entry_ref[...]).T
+    owner = lanes((1, N)) // 8
     for level in range(levels):
-        total = None
+        total, row = None, jnp.zeros((1, N), F32)
         for d in range(5):
             other = level + d - 2
             if 0 <= other < levels:
                 term = taps_ref[d, level] * values_ref[other]
                 total = term if total is None else total + term
+                row = jnp.where(owner == other, taps_ref[d, level], row)
         out_ref[level] = total
-
-
-def final_kernel(taps_ref, values_ref, slots_ref, entry_ref, out_ref, enter):
-    levels = out_ref.shape[0]
+        wide_ref[level] = wide_left(turned * row)
+
+
+def final_kernel(values_ref, wide_ref, slots_ref, out_hbm, enter, whole, sems):
+    levels = enter.shape[0]
     left = lanes((4, N)) < HALF
     for level in range(levels):
         a, b = slots_ref[2 * level], slots_ref[2 * level + 1]
         enter[level, 0:4, :] = jnp.where(left, a, pltpu.roll(b, HALF, 1))
         enter[level, 4:8, :] = jnp.where(left, pltpu.roll(a, HALF, 1), b)
-    for level in range(levels):
-        weights, states = [], []
-        for d in range(5):
-            other = level + d - 2
-            if 0 <= other < levels:
-                weights.append(taps_ref[d, level] * entry_ref[other])
-                states.append(enter[other])
-        weights = jnp.concatenate(weights, 0)
-        states = jnp.concatenate(states, 0)
-        out_ref[level] = values_ref[level] + dot3(weights, states, TN)
+    right = wide_right(flat(enter[...]))
+    copies = []
+    for level in range(0, levels, CHUNK):
+        part = pl.ds(level, CHUNK)
+        added = wide_dot(flat(wide_ref[part]), right).reshape(CHUNK, N, N)
+        whole[part] = values_ref[part] + added
+        if (level + CHUNK) % SENT == 0:
+            part = pl.ds(level + CHUNK - SENT, SENT)
+            copies.append(
+                pltpu.make_async_copy(whole.at[part], out_hbm.at[part], sems.at[level // SENT])
+            )
+            copies[-1].start()
+    for copy in copies:
+        copy.wait()
 
 
 VM = pl.BlockSpec(memory_space=pltpu.VMEM)
 SM = pl.BlockSpec(memory_space=pltpu.SMEM)
-
-
-def call(kernel, shapes, args, scratch=(), flops=0, smem=()):
-    outs = [jax.ShapeDtypeStruct(shape, F32) for shape in shapes]
+HB = pl.BlockSpec(memory_space=pltpu.HBM)
+
+
+def call(kernel, shapes, args, scratch=(), ins=None, out=VM, sems=0, types=None, grant=GRANT):
+    types = types or [F32] * len(shapes)
+    outs = [jax.ShapeDtypeStruct(shape, dtype) for shape, dtype in zip(shapes, types)]
     moved = 4 * sum(x.size for x in list(args) + outs)
-    result = pl.pallas_call(
+    scratch = [pltpu.VMEM(shape, F32) for shape in scratch]
+    if sems:
+        scratch.append(pltpu.SemaphoreType.DMA((sems,)))
+    return pl.pallas_call(
         kernel,
         out_shape=outs if len(outs) > 1 else outs[0],
-        in_specs=[SM if k in smem else VM for k in range(len(args))],
-        out_specs=[VM] * len(outs) if len(outs) > 1 else VM,
-        scratch_shapes=[pltpu.VMEM(shape, F32) for shape in scratch],
-        compiler_params=pltpu.CompilerParams(vmem_limit_bytes=GRANT),
-        cost_estimate=pl.CostEstimate(flops=flops, bytes_accessed=moved, transcendentals=0),
+        in_specs=ins or [VM] * len(args),
+        out_specs=[out] * len(outs) if len(outs) > 1 else out,
+        scratch_shapes=scratch,
+        compiler_params=pltpu.CompilerParams(vmem_limit_bytes=grant),
+        cost_estimate=pl.CostEstimate(flops=0, bytes_accessed=moved, transcendentals=0),
     )(*args)
-    return result
 
 
 def exchange(value, axis):
@@ -389,7 +492,15 @@
     table = (N, levels, N)
     bind = functools.partial
 
-    closing = call(states_x_kernel, [small], (scale_x, control), [small])
+    closing = call(
+        states_x_kernel,
+        [small],
+        (scale_x, control),
+        [(levels, N), full, (8 * levels, N)],
+        ins=[HB, HB],
+        sems=2,
+        grant=60 << 20,
+    )
     closing = exchange(closing, "gx")
     link = call(link_x_kernel, [(8 * nx, N)], (scale_x,), [(nx, N), (14, nx, N)])
     filter_x = call(bind(filter_kernel, "gx"), [full], (scale_x,), [table, table])
@@ -406,10 +517,23 @@
     filter_y = call(bind(filter_kernel, None), [full], (scale_y,), [table, table])
     local = call(local_y_kernel, [full], (local, enter_x, entry_x, filter_y))
 
-    slots = call(apply_y_kernel, [(ny, 4, N)], (slots,), [(14, ny, N), (ny, 8, N)])
-    slots = exchange(slots, "gy")
-    local = call(vertical_kernel, [full], (taps, local), smem=(0,))
-    return call(final_kernel, [full], (taps, local, slots, entry_y), [small], smem=(0,))
+    slots = call(
+        apply_y_kernel,
+        [(4 * ny, N)],
+        (slots.reshape(8 * ny, N),),
+        [(ny, N), (4, ny, N), (8, ny, N), (4, ny, N), (8, 8, N), (4, 8, N)],
+    )
+    slots = exchange(slots.reshape(ny, 4, N), "gy")
+    local, wide = call(
+        vertical_kernel,
+        [full, (levels, N, 2 * N)],
+        (taps, local, entry_y),
+        ins=[SM, VM, VM],
+        types=[F32, BF16],
+    )
+    return call(
+        final_kernel, [full], (local, wide, slots), [small, full], out=HB, sems=levels // SENT
+    )
 
 
 def solution(mesh):

time: 73.6 us -> 70.2 us (0.954)
  local copies, waits for them, and re-layouts: 2.15 us -> 0.03 us
  Pallas kernels: 18.7 us -> 17.5 us
    unnamed x12 -> x8, local copies, waits for them, and re-layouts: 2.15 us -> 0.03 us
    pallas_call x12, Pallas kernels: 18.7 us -> 17.5 us  [call(): pl.pallas_call(kernel, out_shape=outs if len(outs) > 1 else outs[0], in_s...]
  transfers between devices with their start and end apart: 3 -> 3, of which waited for: 3 -> 3; matrix products, arithmetic and copies ran while one was open for 0% -> 0% of each run, Pallas kernels for 15% -> 16%
where the time goes in v1:
time: 70.2 us; the launch traced here: 69.4 us
  starting transfers between devices  19.8 us (28%)
  blocking collectives  18.6 us (26%)
  Pallas kernels  17.5 us (25%)
  waiting for transfers between devices  13.3 us (19%)
    all_to_all x3, starting transfers between devices, exchange(): return lax.all_to_all(value, axis, 0, 0, tiled=True)  19.8 us
    all_to_all x1, blocking collectives, exchange(): return lax.all_to_all(value, axis, 0, 0, tiled=True)  18.6 us
    pallas_call x12, Pallas kernels, call(): pl.pallas_call(kernel, out_shape=outs if len(outs) > 1 else outs[0], in_s...  17.5 us
    all_to_all x3, waiting for transfers between devices, exchange(): return lax.all_to_all(value, axis, 0, 0, tiled=True)  13.3 us
  transfers between devices with their start and end apart: 3, of which 3 were waited for; matrix products, arithmetic and copies ran while one was open for 0% of the time, Pallas kernels for 16%

profile of v1, /device:TPU:1, one launch (start us, length us, event | category | flops | bytes accessed | tf_op | source)
XLA Modules:
  0.0 69.4 jit_solution(17176359319916521053)
XLA Ops:
  0.0 2.8 %shard_map.50 = f32[16,8,128]{2,1,0:T(8,128)} custom-call(f32[16,2048]{1,0:T(8,128)} %scale_hbm.1, f32[16,128,128]{2,1,0:T(8,128)} %control_hbm.1), custom_call_target="tpu_custom_call" | custom-call | bytes 1245184 | tf_op jit(solution)/shard_map/pallas_call | solution.py:473
  2.8 0.0 copy-start
  2.8 12.0 %all-to-all-start = ((f32[16,8,128]{2,1,0:T(8,128)}), f32[16,8,128]{2,1,0:T(8,128)S(1)}, u32[]{:S(2)}, u32[]{:S(2)}) async-start(f32[16,8,128]{2,1,0:T(8,128)} %shard_map.50), calls=%async_computation | async-start | bytes 131072 | tf_op jit(solution)/shard_map/all_to_all | solution.py:485
  14.8 1.0 %shard_map.49.link_ref = f32[128,128]{1,0:T(8,128)S(1)} custom-call(f32[16,2048]{1,0:T(8,128)S(1)} %copy-done.1), custom_call_target="tpu_custom_call" | custom-call | bytes 196608 | tf_op jit(solution)/shard_map/pallas_call | solution.py:473
  15.8 6.8 %all-to-all-done.states_ref = f32[16,8,128]{2,1,0:T(8,128)S(1)} async-done(((f32[16,8,128]{2,1,0:T(8,128)}), f32[16,8,128]{2,1,0:T(8,128)S(1)}, u32[]{:S(2)}, u32[]{:S(2)}) %all-to-all-start) | async-done | bytes 65568 | tf_op jit(solution)/shard_map/all_to_all | solution.py:485
  22.5 0.8 %shard_map.51 = f32[16,8,128]{2,1,0:T(8,128)} custom-call(f32[128,128]{1,0:T(8,128)S(1)} %shard_map.49.link_ref, f32[16,8,128]{2,1,0:T(8,128)S(1)} %all-to-all-done.states_ref), custom_call_target="tpu_custom_call" | custom-call | bytes 196608 | tf_op jit(solution)/shard_map/pallas_call | solution.py:473
  23.3 3.4 %all-to-all-start.1 = ((f32[16,8,128]{2,1,0:T(8,128)}), f32[16,8,128]{2,1,0:T(8,128)S(1)}, u32[]{:S(2)}, u32[]{:S(2)}) async-start(f32[16,8,128]{2,1,0:T(8,128)} %shard_map.51), calls=%async_computation.1 | async-start | bytes 131072 | tf_op jit(solution)/shard_map/all_to_all | solution.py:485
  26.8 0.0 copy-start.2
  26.8 2.9 %shard_map.47.filter_ref = f32[16,128,128]{2,1,0:T(8,128)S(1)} custom-call(f32[16,2048]{1,0:T(8,128)S(1)} %copy-done.1), custom_call_target="tpu_custom_call" | custom-call | bytes 1179648 | tf_op jit(solution)/shard_map/pallas_call | solution.py:473
  29.7 0.0 copy-done.2
  29.7 1.0 %shard_map.46 = (f32[16,8,128]{2,1,0:T(8,128)S(1)}, f32[16,128]{1,0:T(8,128)S(1)}, f32[16,8,128]{2,1,0:T(8,128)S(1)}, f32[16,8,128]{2,1,0:T(8,128)S(1)}, f32[16,128]{1,0:T(8,128)S(1)}) custom-call(f32[16,2048]{1,0:T(8,128)S(1)} %copy-done.1, f32[16,128]{1,0:T(8,128)S(1)} %copy-done.2), custom_call_target="tpu_custom_call" | custom-call | bytes 352256 | tf_op jit(solution)/shard_map/pallas_call | solution.py:473
  30.7 1.1 %shard_map.48 = (f32[16,128,128]{2,1,0:T(8,128)S(1)}, f32[16,8,128]{2,1,0:T(8,128)S(1)}) custom-call(f32[16,128,128]{2,1,0:T(8,128)S(1)} %copy-done, f32[16,128]{1,0:T(8,128)S(1)} %get-tuple-element.14.gain_ref, f32[16,128,128]{2,1,0:T(8,128)S(1)} %shard_map.47.filter_ref, f32[16,8,128]{2,1,0:T(8,128)S(1)} %get-tuple-element.15.extract_ref), custom_call_target="tpu_custom_call" | custom-call | bytes 3284992 | tf_op jit(solution)/shard_map/pallas_call | solution.py:473
  31.8 2.7 %all-to-all-done.1.enter_ref = f32[16,8,128]{2,1,0:T(8,128)S(1)} async-done(((f32[16,8,128]{2,1,0:T(8,128)}), f32[16,8,128]{2,1,0:T(8,128)S(1)}, u32[]{:S(2)}, u32[]{:S(2)}) %all-to-all-start.1) | async-done | bytes 65568 | tf_op jit(solution)/shard_map/all_to_all | solution.py:485
  34.6 0.4 shard_map.55
  35.0 18.6 %all_to_all.20 = f32[32,8,128]{2,1,0:T(8,128)S(1)} all-to-all(f32[32,8,128]{2,1,0:T(8,128)S(1)} %shard_map.55), channel_id=1, replica_groups=mesh['gx'=16,'gy'=32] {'gy'}, dimensions={0} | all-to-all | bytes 262144 | tf_op jit(solution)/shard_map/all_to_all | solution.py:485
  53.6 1.0 %shard_map.56 = f32[128,128]{1,0:T(8,128)} custom-call(f32[256,128]{1,0:T(8,128)S(1)} %bitcast.2), custom_call_target="tpu_custom_call" | custom-call | bytes 196608 | tf_op jit(solution)/shard_map/pallas_call | solution.py:473
  54.6 4.4 %all-to-all-start.3 = ((f32[32,4,128]{2,1,0:T(4,128)}), f32[32,4,128]{2,1,0:T(4,128)S(1)}, u32[]{:S(2)}, u32[]{:S(2)}) async-start(f32[32,4,128]{2,1,0:T(4,128)} %bitcast.1), calls=%async_computation.3 | async-start | bytes 131072 | tf_op jit(solution)/shard_map/all_to_all | solution.py:485
  59.0 2.9 %shard_map.52.filter_ref = f32[16,128,128]{2,1,0:T(8,128)S(1)} custom-call(f32[16,128]{1,0:T(8,128)S(1)} %copy-done.2), custom_call_target="tpu_custom_call" | custom-call | bytes 1056768 | tf_op jit(solution)/shard_map/pallas_call | solution.py:473
  61.9 0.0 copy-start.3
  61.9 1.2 %shard_map.53.values_ref = f32[16,128,128]{2,1,0:T(8,128)S(1)} custom-call(f32[16,128,128]{2,1,0:T(8,128)S(1)} %get-tuple-element.16.base_ref, f32[16,8,128]{2,1,0:T(8,128)S(1)} %all-to-all-done.1.enter_ref, f32[16,8,128]{2,1,0:T(8,128)S(1)} %get-tuple-element.17.entry_ref, f32[16,128,128]{2,1,0:T(8,128)S(1)} %shard_map.52.filter_ref), custom_call_target="tpu_custom_call" | custom-call | bytes 3276800 | tf_op jit(solution)/shard_map/pallas_call | solution.py:473
  63.1 0.0 copy-done.3
  63.1 1.1 %shard_map.54 = (f32[16,128,128]{2,1,0:T(8,128)S(1)}, bf16[16,128,256]{2,1,0:T(8,128)(2,1)S(1)}) custom-call(f32[5,16]{1,0:T(8,128)S(1)} %copy-done.3, f32[16,128,128]{2,1,0:T(8,128)S(1)} %shard_map.53.values_ref, f32[16,8,128]{2,1,0:T(8,128)S(1)} %get-tuple-element.18.entry_ref), custom_call_target="tpu_custom_call" | custom-call | bytes 4260160 | tf_op jit(solution)/shard_map/pallas_call | solution.py:473
  64.2 3.8 %all-to-all-done.3.slots_ref = f32[32,4,128]{2,1,0:T(4,128)S(1)} async-done(((f32[32,4,128]{2,1,0:T(4,128)}), f32[32,4,128]{2,1,0:T(4,128)S(1)}, u32[]{:S(2)}, u32[]{:S(2)}) %all-to-all-start.3) | async-done | bytes 65568 | tf_op jit(solution)/shard_map/all_to_all | solution.py:485
  68.0 1.4 %shard_map.57 = f32[16,128,128]{2,1,0:T(8,128)} custom-call(f32[16,128,128]{2,1,0:T(8,128)S(1)} %get-tuple-element.19.values_ref, bf16[16,128,256]{2,1,0:T(8,128)(2,1)S(1)} %get-tuple-element.20.wide_ref, f32[32,4,128]{2,1,0:T(4,128)S(1)} %all-to-all-done.3.slots_ref), custom_call_target="tpu_custom_call" | custom-call | bytes 4259840 | tf_op jit(solution)/shard_map/pallas_call | solution.py:473
  (3 shorter events, 0.0 us)
Async XLA Ops:
  0.0 14.8 %copy-start.1 = (f32[16,2048]{1,0:T(8,128)S(1)}, f32[16,2048]{1,0:T(8,128)}, u32[]{:S(2)}) copy-start(f32[16,2048]{1,0:T(8,128)} %scale_hbm.1) | copy-start | bytes 393220
  2.8 27.9 %copy-start = (f32[16,128,128]{2,1,0:T(8,128)S(1)}, f32[16,128,128]{2,1,0:T(8,128)}, u32[]{:S(2)}) copy-start(f32[16,128,128]{2,1,0:T(8,128)} %control_hbm.1) | copy-start | bytes 3145732
  2.8 19.7 %all-to-all-start = ((f32[16,8,128]{2,1,0:T(8,128)}), f32[16,8,128]{2,1,0:T(8,128)S(1)}, u32[]{:S(2)}, u32[]{:S(2)}) async-start(f32[16,8,128]{2,1,0:T(8,128)} %shard_map.50), calls=%async_computation | async-start | bytes 131072 | tf_op jit(solution)/shard_map/all_to_all | solution.py:485
  23.3 11.2 %all-to-all-start.1 = ((f32[16,8,128]{2,1,0:T(8,128)}), f32[16,8,128]{2,1,0:T(8,128)S(1)}, u32[]{:S(2)}, u32[]{:S(2)}) async-start(f32[16,8,128]{2,1,0:T(8,128)} %shard_map.51), calls=%async_computation.1 | async-start | bytes 131072 | tf_op jit(solution)/shard_map/all_to_all | solution.py:485
  26.8 2.9 %copy-start.2 = (f32[16,128]{1,0:T(8,128)S(1)}, f32[16,128]{1,0:T(8,128)}, u32[]{:S(2)}) copy-start(f32[16,128]{1,0:T(8,128)} %scale_ref.5) | copy-start | bytes 24580
  54.6 13.4 %all-to-all-start.3 = ((f32[32,4,128]{2,1,0:T(4,128)}), f32[32,4,128]{2,1,0:T(4,128)S(1)}, u32[]{:S(2)}, u32[]{:S(2)}) async-start(f32[32,4,128]{2,1,0:T(4,128)} %bitcast.1), calls=%async_computation.3 | async-start | bytes 131072 | tf_op jit(solution)/shard_map/all_to_all | solution.py:485
  61.9 1.2 %copy-start.3 = (f32[5,16]{1,0:T(8,128)S(1)}, f32[5,16]{1,0:T(8,128)}, u32[]{:S(2)}) copy-start(f32[5,16]{1,0:T(8,128)} %taps_ref.1) | copy-start | bytes 964

commit v2 on v1

--- a/solution.py
+++ b/solution.py
@@ -185,84 +185,134 @@
     return value.reshape(value.shape[0] * value.shape[1], value.shape[2])
 
 
-def states_x_kernel(scale_hbm, control_hbm, out_ref, scale_ref, control_ref, weights, sems):
-    levels = out_ref.shape[0]
+def combine(first, second):
+    t, r = first
+    grown = congruence(t, second[1])
+    return poly(t, second[0]), {key: r[key] + grown[key] for key in r}
+
+
+def block_maps(scale_ref, table):
+    levels = scale_ref.shape[0]
+    per = N // levels
+    out = []
+    for h in range(scale_ref.shape[1] // (per * N)):
+        rows = [scale_ref[:, (h * per + j) * N:(h * per + j + 1) * N] for j in range(per)]
+        turned = jnp.concatenate(rows, 0).T
+        table[h] = jnp.exp(-1.0 / turned)
+        t, r = None, None
+        for i in range(N // 8):
+            p = table[h, pl.ds(i, 8, stride=N // 8), :]
+            q = 1.0 - p
+            if t is None:
+                t = geometric(p, q)
+            else:
+                t = [p * value for value in t]
+                for k in range(1, 4):
+                    t[k] = t[k] + q * t[k - 1]
+            lead = [q / p * value for value in t]
+            grown = {key: lead[key[0]] * t[key[1]] for key in COEFS}
+            r = grown if r is None else {key: r[key] + grown[key] for key in COEFS}
+        for d in (1, 2, 4):
+            move = functools.partial(pltpu.roll, shift=8 - d, axis=0)
+            t, r = combine((t, r), ([move(v) for v in t], {key: move(v) for key, v in r.items()}))
+        out.append(([v[0:1] for v in t], {key: v[0:1] for key, v in r.items()}))
+    return out
+
+
+def return_after(maps, me, levels):
+    per = N // levels
+    block = lanes((1, N)) // levels
+    halves = []
+    for h, (t, r) in enumerate(maps):
+        after = block + h * per > me
+        t = [jnp.where(after, t[k], ones_first(k)) for k in range(4)]
+        r = {key: jnp.where(after, v, 0.0) for key, v in r.items()}
+        for d in (1, 2, 4):
+            move = functools.partial(pltpu.roll, shift=N - levels * d, axis=1)
+            t, r = combine((t, r), ([move(v) for v in t], {key: move(v) for key, v in r.items()}))
+        halves.append((t, r))
+    r = combine(halves[0], halves[1])[1]
+    rows = [r[key] for key in COEFS]
+    rows = jnp.concatenate(rows + [rows[0]] * (16 - len(rows)), 0).T
+    return {
+        key: jnp.broadcast_to(rows[:levels, m:m + 1], (levels, N)) for m, key in enumerate(COEFS)
+    }
+
+
+def states_x_kernel(scale_hbm, control_hbm, out_ref, scale_ref, control_ref, weights, table, sems):
+    levels = scale_ref.shape[0]
+    blocks = out_ref.shape[0]
     me = lax.axis_index("gx")
-    first = pltpu.make_async_copy(
-        scale_hbm.at[:, pl.ds(pl.multiple_of(me * N, N), N)], scale_ref, sems.at[0]
-    )
+    first = pltpu.make_async_copy(scale_hbm, scale_ref, sems.at[0])
     second = pltpu.make_async_copy(control_hbm, control_ref, sems.at[1])
     first.start()
     second.start()
     first.wait()
-    scale = scale_ref[...]
+    back_map = return_after(block_maps(scale_ref, table), me, levels)
+    scale = own_scale("gx", scale_ref)
     p, q = poles(scale)
     t, r = suffix_scan(p, q)
     before = prefix_scan(p, q)
     f, b = extraction(p, q, t, r, before)
+    own = [jnp.broadcast_to(t[k][:, 0:1], (levels, N)) for k in range(4)]
+    returned = poly(own, return_map(back_map, f))
+    b = [b[k] + returned[k] for k in range(4)]
     amplitude = jnp.sqrt(8.0 * scale)
     for k in range(4):
-        weights[pl.ds(k, levels, stride=8), :] = f[k] * amplitude
-        weights[pl.ds(4 + k, levels, stride=8), :] = b[k] * amplitude
+        weights[pl.ds(k, levels, stride=4), :] = f[k] * amplitude
+        weights[pl.ds(4 * levels + k, levels, stride=4), :] = b[k] * amplitude
     right = wide_right(weights[...].T)
-    owner = lanes((N, N)) // 8
+    owner = (lanes((N, N)) % (4 * levels)) // 4
     total = jnp.zeros((N, N), F32)
     second.wait()
     for level in range(0, levels, CHUNK):
         every = wide_dot(wide_left(flat(control_ref[level:level + CHUNK])), right)
         for k in range(CHUNK):
             total = jnp.where(owner == level + k, every[k * N:(k + 1) * N], total)
-    out_ref[...] = total.T.reshape(levels, 8, N)
-
-
-def link_x_kernel(scale_ref, out_ref, gathered, spread):
-    blocks = out_ref.shape[0] // 8
+    weights[...] = total.T
+    for j in range(blocks):
+        start = pl.multiple_of(jnp.where(me > j, 4 * levels, 0), 4 * levels)
+        out_ref[j] = weights[pl.ds(start, 4 * levels), :]
+
+
+def links_x_kernel(scale_ref, link_ref, table):
+    levels = scale_ref.shape[0]
+    blocks = scale_ref.shape[1] // N
+    per = N // levels
     me = lax.axis_index("gx")
-    level = lax.broadcasted_iota(jnp.int32, (scale_ref.shape[0], N), 0)
+    maps = block_maps(scale_ref, table)
+    back_map = return_after(maps, me, levels)
+    for m, key in enumerate(COEFS):
+        link_ref[4 * blocks + 4 + m] = back_map[key]
+    rows = [t[k] for t, _ in maps for k in range(4)]
+    turned = jnp.concatenate(rows, 0).T
+
+    def block(j):
+        h, i = j // per, j % per
+        part = turned[i * levels:(i + 1) * levels]
+        return [
+            jnp.broadcast_to(part[:, 4 * h + k:4 * h + k + 1], (levels, N)) for k in range(4)
+        ]
+
+    unit = [jnp.full((levels, N), ones_first(k), F32) for k in range(4)]
+    own = [jnp.zeros((levels, N), F32)] * 4
+    current = unit
+    for j in reversed(range(blocks)):
+        t = block(j)
+        for k in range(4):
+            link_ref[4 * j + k] = jnp.where(me > j, current[k], 0.0)
+        moved = poly(t, current)
+        current = [jnp.where(me > j, moved[k], unit[k]) for k in range(4)]
+        own = [jnp.where(me == j, t[k], own[k]) for k in range(4)]
+    current = unit
     for j in range(blocks):
-        block = jnp.where(level == me, scale_ref[:, j * N:(j + 1) * N], 0.0)
-        gathered[j:j + 1, :] = jnp.sum(block, axis=0, keepdims=True)
-    p, q = poles(gathered[...])
-    t, r = suffix_scan(p, q)
-    for k in range(4):
-        spread[k] = jnp.broadcast_to(t[k][:, 0:1], (blocks, N))
-    for m, key in enumerate(COEFS):
-        spread[4 + m] = jnp.broadcast_to(r[key][:, 0:1], (blocks, N))
-    lane = lanes((1, N))
-    run_links(
-        blocks,
-        lambda j, k: (lane == 8 * j + k).astype(F32),
-        spread,
-        lambda j, k, value: out_ref.__setitem__((pl.ds(8 * j + k, 1), slice(None)), value),
-    )
-
-
-def run_links(blocks, source, spread, store):
-    zero = jnp.zeros((1, N), F32)
-    s = [zero] * 4
-    returns = []
-    for j in range(blocks):
-        t = [spread[k, j:j + 1, :] for k in range(4)]
-        r = {key: spread[4 + m, j:j + 1, :] for m, key in enumerate(COEFS)}
+        t = block(j)
         for k in range(4):
-            store(j, k, s[k])
-        back = return_map(r, s)
-        returns.append([back[k] + source(j, 4 + k) for k in range(4)])
-        moved = poly(t, s)
-        s = [moved[k] + source(j, k) for k in range(4)]
-    e = [zero] * 4
-    for j in reversed(range(blocks)):
-        t = [spread[k, j:j + 1, :] for k in range(4)]
-        for k in range(4):
-            store(j, 4 + k, e[k])
-        moved = poly(t, e)
-        e = [moved[k] + returns[j][k] for k in range(4)]
-
-
-def apply_x_kernel(link_ref, states_ref, out_ref):
-    blocks = out_ref.shape[0]
-    flat = states_ref[...].reshape(blocks * 8, N)
-    out_ref[...] = dot3(link_ref[...], flat, NN).reshape(blocks, 8, N)
+            link_ref[4 * j + k] = link_ref[4 * j + k] + jnp.where(me < j, current[k], 0.0)
+        moved = poly(t, current)
+        current = [jnp.where(me < j, moved[k], unit[k]) for k in range(4)]
+    for k in range(4):
+        link_ref[4 * blocks + k] = own[k]
 
 
 def filter_kernel(axis, scale_ref, local_ref, spread, middle):
@@ -289,15 +339,15 @@
         middle[i] = state[3]
         return tuple(state)
 
-    lax.fori_loop(0, N, forward, (zero,) * 4, unroll=8)
+    lax.fori_loop(0, N, forward, (zero,) * 4, unroll=16)
 
     def backward(k, state):
         i = N - 1 - k
         state = advance(spread[i], state, middle[i])
-        local_ref[:, pl.ds(i, 1), :] = (state[3] * column).reshape(levels, 1, N)
+        local_ref[pl.ds(i, levels, stride=N), :] = state[3] * column
         return tuple(state)
 
-    lax.fori_loop(0, N, backward, (zero,) * 4, unroll=8)
+    lax.fori_loop(0, N, backward, (zero,) * 4, unroll=16)
 
 
 def tables_kernel(scale_x_ref, scale_y_ref, entry_x_ref, gain_x_ref, extract_ref, entry_y_ref, coef_ref):
@@ -333,9 +383,29 @@
         base_ref[level] = dot3(extract_ref[level], g, NN)
 
 
-def states_y_kernel(enter_ref, entry_ref, extract_ref, base_ref, coef_ref, out_ref):
+def states_y_kernel(
+    sent_ref, link_ref, entry_ref, extract_ref, base_ref, coef_ref, out_ref, enter_ref
+):
     levels = base_ref.shape[0]
-    corner = dot3(flat(extract_ref[...]), flat(enter_ref[...]), NT)
+    blocks = sent_ref.shape[0] // (4 * levels)
+    me = lax.axis_index("gx")
+    zero = jnp.zeros((levels, N), F32)
+    s, e = [zero] * 4, [zero] * 4
+    for j in range(blocks):
+        sent = [sent_ref[pl.ds(4 * levels * j + k, levels, stride=4), :] for k in range(4)]
+        moved = poly([link_ref[4 * j + k] for k in range(4)], sent)
+        s = [jnp.where(me > j, s[k] + moved[k], s[k]) for k in range(4)]
+        e = [jnp.where(me < j, e[k] + moved[k], e[k]) for k in range(4)]
+    moved = poly([link_ref[4 * blocks + k] for k in range(4)], s)
+    first = 4 * levels * me
+    after = [
+        moved[k] + sent_ref[pl.ds(first + k, levels, stride=4), :] for k in range(4)
+    ]
+    back = return_map({key: link_ref[4 * blocks + 4 + m] for m, key in enumerate(COEFS)}, after)
+    for k in range(4):
+        enter_ref[pl.ds(k, levels, stride=8), :] = s[k]
+        enter_ref[pl.ds(4 + k, levels, stride=8), :] = e[k] + back[k]
+    corner = dot3(flat(extract_ref[...]), enter_ref[...], NT)
     here = lax.broadcasted_iota(jnp.int32, (N, N), 0) // 8 == lanes((N, N)) // 8
     corner = jnp.where(here, corner, 0.0)
     states = flat(base_ref[...]) + dot3(corner, flat(entry_ref[...]), NN)
@@ -494,28 +564,37 @@
 
     closing = call(
         states_x_kernel,
-        [small],
+        [(nx, 4 * levels, N)],
         (scale_x, control),
-        [(levels, N), full, (8 * levels, N)],
+        [(levels, N * nx), full, (N, N), (levels * nx // N, N, N)],
         ins=[HB, HB],
         sems=2,
         grant=60 << 20,
     )
     closing = exchange(closing, "gx")
-    link = call(link_x_kernel, [(8 * nx, N)], (scale_x,), [(nx, N), (14, nx, N)])
-    filter_x = call(bind(filter_kernel, "gx"), [full], (scale_x,), [table, table])
-
-    enter_x = call(apply_x_kernel, [small], (link, closing))
-    enter_x = exchange(enter_x, "gx")
+    filter_x = call(bind(filter_kernel, "gx"), [(levels * N, N)], (scale_x,), [table, table])
+    links = call(
+        links_x_kernel,
+        [(4 * nx + 4 + len(COEFS), levels, N)],
+        (scale_x,),
+        [(levels * nx // N, N, N)],
+    )
     entry_x, gain_x, extract_y, entry_y, coefs = call(
         tables_kernel, [small, (levels, N), small, small, (levels, N)], (scale_x, scale_y)
     )
-    local, base = call(local_x_kernel, [full, small], (control, gain_x, filter_x, extract_y))
-
-    slots = call(states_y_kernel, [(ny, 8, N)], (enter_x, entry_x, extract_y, base, coefs))
+    local, base = call(
+        local_x_kernel, [full, small], (control, gain_x, filter_x.reshape(full), extract_y)
+    )
+
+    slots, enter_x = call(
+        states_y_kernel,
+        [(ny, 8, N), (8 * levels, N)],
+        (closing.reshape(4 * levels * nx, N), links, entry_x, extract_y, base, coefs),
+    )
+    enter_x = enter_x.reshape(small)
     slots = exchange(slots, "gy")
-    filter_y = call(bind(filter_kernel, None), [full], (scale_y,), [table, table])
-    local = call(local_y_kernel, [full], (local, enter_x, entry_x, filter_y))
+    filter_y = call(bind(filter_kernel, None), [(levels * N, N)], (scale_y,), [table, table])
+    local = call(local_y_kernel, [full], (local, enter_x, entry_x, filter_y.reshape(full)))
 
     slots = call(
         apply_y_kernel,

time: 70.2 us -> 68.2 us (0.972)
  starting transfers between devices: 19.8 us -> 15.8 us
  waiting for transfers between devices: 13.3 us -> 16.5 us
  Pallas kernels: 17.5 us -> 16 us
  blocking collectives: 18.6 us -> 19.4 us
    all_to_all x3 -> x2, starting transfers between devices: 19.8 us -> 15.8 us  [exchange(): return lax.all_to_all(value, axis, 0, 0, tiled=True)]
    all_to_all x3 -> x2, waiting for transfers between devices: 13.3 us -> 16.5 us  [exchange(): return lax.all_to_all(value, axis, 0, 0, tiled=True)]
    pallas_call x12 -> x11, Pallas kernels: 17.5 us -> 16 us  [call(): pl.pallas_call(kernel, out_shape=outs if len(outs) > 1 else outs[0], in_s...]
    all_to_all x1, blocking collectives: 18.6 us -> 19.4 us  [exchange(): return lax.all_to_all(value, axis, 0, 0, tiled=True)]
  transfers between devices with their start and end apart: 3 -> 2, of which waited for: 3 -> 2; matrix products, arithmetic and copies ran while one was open for 0% -> 0% of each run, Pallas kernels for 16% -> 14%
where the time goes in v2:
time: 68.2 us; the launch traced here: 67.9 us
  blocking collectives  19.4 us (28%)
  waiting for transfers between devices  16.5 us (24%)
  Pallas kernels  16 us (23%)
  starting transfers between devices  15.8 us (23%)
    all_to_all x1, blocking collectives, exchange(): return lax.all_to_all(value, axis, 0, 0, tiled=True)  19.4 us
    all_to_all x2, waiting for transfers between devices, exchange(): return lax.all_to_all(value, axis, 0, 0, tiled=True)  16.5 us
    pallas_call x11, Pallas kernels, call(): pl.pallas_call(kernel, out_shape=outs if len(outs) > 1 else outs[0], in_s...  16 us
    all_to_all x2, starting transfers between devices, exchange(): return lax.all_to_all(value, axis, 0, 0, tiled=True)  15.8 us
  transfers between devices with their start and end apart: 2, of which 2 were waited for; matrix products, arithmetic and copies ran while one was open for 0% of the time, Pallas kernels for 14%

profile of v2, /device:TPU:1, one launch (start us, length us, event | category | flops | bytes accessed | tf_op | source)
XLA Modules:
  0.0 67.9 jit_solution(17532356122720025211)
XLA Ops:
  0.0 3.5 %shard_map.49 = f32[16,64,128]{2,1,0:T(8,128)} custom-call(f32[16,2048]{1,0:T(8,128)} %scale_ref.4, f32[16,128,128]{2,1,0:T(8,128)} %control_hbm.1), custom_call_target="tpu_custom_call" | custom-call | bytes 1703936 | tf_op jit(solution)/shard_map/pallas_call | solution.py:543
  3.5 0.0 copy-start.1
  3.5 12.0 %all-to-all-start = ((f32[16,64,128]{2,1,0:T(8,128)}), f32[16,64,128]{2,1,0:T(8,128)S(1)}, u32[]{:S(2)}, u32[]{:S(2)}) async-start(f32[16,64,128]{2,1,0:T(8,128)} %shard_map.49), calls=%async_computation | async-start | bytes 1048576 | tf_op jit(solution)/shard_map/all_to_all | solution.py:555
  15.5 0.0 copy-done.1
  15.5 0.0 copy-start
  15.5 2.0 %shard_map.47 = f32[2048,128]{1,0:T(8,128)S(1)} custom-call(f32[16,2048]{1,0:T(8,128)S(1)} %copy-done.1), custom_call_target="tpu_custom_call" | custom-call | bytes 1179648 | tf_op jit(solution)/shard_map/pallas_call | solution.py:543
  17.5 0.0 copy-start.2
  17.5 1.1 %shard_map.50.link_ref = f32[78,16,128]{2,1,0:T(8,128)S(1)} custom-call(f32[16,2048]{1,0:T(8,128)S(1)} %copy-done.1), custom_call_target="tpu_custom_call" | custom-call | bytes 770048 | tf_op jit(solution)/shard_map/pallas_call | solution.py:543
  18.7 0.0 copy-done.2
  18.7 1.0 %shard_map.46 = (f32[16,8,128]{2,1,0:T(8,128)S(1)}, f32[16,128]{1,0:T(8,128)S(1)}, f32[16,8,128]{2,1,0:T(8,128)S(1)}, f32[16,8,128]{2,1,0:T(8,128)S(1)}, f32[16,128]{1,0:T(8,128)S(1)}) custom-call(f32[16,2048]{1,0:T(8,128)S(1)} %copy-done.1, f32[16,128]{1,0:T(8,128)S(1)} %copy-done.2), custom_call_target="tpu_custom_call" | custom-call | bytes 352256 | tf_op jit(solution)/shard_map/pallas_call | solution.py:543
  19.7 0.0 copy-done
  19.7 1.1 %shard_map.48 = (f32[16,128,128]{2,1,0:T(8,128)S(1)}, f32[16,8,128]{2,1,0:T(8,128)S(1)}) custom-call(f32[16,128,128]{2,1,0:T(8,128)S(1)} %copy-done, f32[16,128]{1,0:T(8,128)S(1)} %get-tuple-element.16.gain_ref, f32[16,128,128]{2,1,0:T(8,128)S(1)} %bitcast.7, f32[16,8,128]{2,1,0:T(8,128)S(1)} %get-tuple-element.17.extract_ref), custom_call_target="tpu_custom_call" | custom-call | bytes 3284992 | tf_op jit(solution)/shard_map/pallas_call | solution.py:543
  20.8 11.8 %all-to-all-done = f32[16,64,128]{2,1,0:T(8,128)S(1)} async-done(((f32[16,64,128]{2,1,0:T(8,128)}), f32[16,64,128]{2,1,0:T(8,128)S(1)}, u32[]{:S(2)}, u32[]{:S(2)}) %all-to-all-start) | async-done | bytes 524320 | tf_op jit(solution)/shard_map/all_to_all | solution.py:555
  32.7 0.6 shard_map.51
  33.3 19.4 %all_to_all.15 = f32[32,8,128]{2,1,0:T(8,128)S(1)} all-to-all(f32[32,8,128]{2,1,0:T(8,128)S(1)} %get-tuple-element.26), channel_id=1, replica_groups=mesh['gx'=16,'gy'=32] {'gy'}, dimensions={0} | all-to-all | bytes 262144 | tf_op jit(solution)/shard_map/all_to_all | solution.py:555
  52.7 1.0 %shard_map.55 = f32[128,128]{1,0:T(8,128)} custom-call(f32[256,128]{1,0:T(8,128)S(1)} %bitcast.9), custom_call_target="tpu_custom_call" | custom-call | bytes 196608 | tf_op jit(solution)/shard_map/pallas_call | solution.py:543
  53.7 3.9 %all-to-all-start.2 = ((f32[32,4,128]{2,1,0:T(4,128)}), f32[32,4,128]{2,1,0:T(4,128)S(1)}, u32[]{:S(2)}, u32[]{:S(2)}) async-start(f32[32,4,128]{2,1,0:T(4,128)} %bitcast.5), calls=%async_computation.2 | async-start | bytes 131072 | tf_op jit(solution)/shard_map/all_to_all | solution.py:555
  57.5 2.0 %shard_map.52 = f32[2048,128]{1,0:T(8,128)S(1)} custom-call(f32[16,128]{1,0:T(8,128)S(1)} %copy-done.2), custom_call_target="tpu_custom_call" | custom-call | bytes 1056768 | tf_op jit(solution)/shard_map/pallas_call | solution.py:543
  59.6 0.0 copy-start.3
  59.6 1.2 %shard_map.53.values_ref = f32[16,128,128]{2,1,0:T(8,128)S(1)} custom-call(f32[16,128,128]{2,1,0:T(8,128)S(1)} %get-tuple-element.18.base_ref, f32[16,8,128]{2,1,0:T(8,128)S(1)} %bitcast.10, f32[16,8,128]{2,1,0:T(8,128)S(1)} %get-tuple-element.19.entry_ref, f32[16,128,128]{2,1,0:T(8,128)S(1)} %bitcast.6), custom_call_target="tpu_custom_call" | custom-call | bytes 3276800 | tf_op jit(solution)/shard_map/pallas_call | solution.py:543
  60.7 0.0 copy-done.3
  60.8 1.1 %shard_map.54 = (f32[16,128,128]{2,1,0:T(8,128)S(1)}, bf16[16,128,256]{2,1,0:T(8,128)(2,1)S(1)}) custom-call(f32[5,16]{1,0:T(8,128)S(1)} %copy-done.3, f32[16,128,128]{2,1,0:T(8,128)S(1)} %shard_map.53.values_ref, f32[16,8,128]{2,1,0:T(8,128)S(1)} %get-tuple-element.23.entry_ref), custom_call_target="tpu_custom_call" | custom-call | bytes 4260160 | tf_op jit(solution)/shard_map/pallas_call | solution.py:543
  61.9 4.6 %all-to-all-done.2.slots_ref = f32[32,4,128]{2,1,0:T(4,128)S(1)} async-done(((f32[32,4,128]{2,1,0:T(4,128)}), f32[32,4,128]{2,1,0:T(4,128)S(1)}, u32[]{:S(2)}, u32[]{:S(2)}) %all-to-all-start.2) | async-done | bytes 65568 | tf_op jit(solution)/shard_map/all_to_all | solution.py:555
  66.5 1.4 %shard_map.56 = f32[16,128,128]{2,1,0:T(8,128)} custom-call(f32[16,128,128]{2,1,0:T(8,128)S(1)} %get-tuple-element.24.values_ref, bf16[16,128,256]{2,1,0:T(8,128)(2,1)S(1)} %get-tuple-element.25.wide_ref, f32[32,4,128]{2,1,0:T(4,128)S(1)} %all-to-all-done.2.slots_ref), custom_call_target="tpu_custom_call" | custom-call | bytes 4259840 | tf_op jit(solution)/shard_map/pallas_call | solution.py:543
Async XLA Ops:
  3.5 12.0 %copy-start.1 = (f32[16,2048]{1,0:T(8,128)S(1)}, f32[16,2048]{1,0:T(8,128)}, u32[]{:S(2)}) copy-start(f32[16,2048]{1,0:T(8,128)} %scale_ref.4) | copy-start | bytes 393220
  3.5 29.2 %all-to-all-start = ((f32[16,64,128]{2,1,0:T(8,128)}), f32[16,64,128]{2,1,0:T(8,128)S(1)}, u32[]{:S(2)}, u32[]{:S(2)}) async-start(f32[16,64,128]{2,1,0:T(8,128)} %shard_map.49), calls=%async_computation | async-start | bytes 1048576 | tf_op jit(solution)/shard_map/all_to_all | solution.py:555
  15.5 4.3 %copy-start = (f32[16,128,128]{2,1,0:T(8,128)S(1)}, f32[16,128,128]{2,1,0:T(8,128)}, u32[]{:S(2)}) copy-start(f32[16,128,128]{2,1,0:T(8,128)} %control_hbm.1) | copy-start | bytes 3145732
  17.5 1.1 %copy-start.2 = (f32[16,128]{1,0:T(8,128)S(1)}, f32[16,128]{1,0:T(8,128)}, u32[]{:S(2)}) copy-start(f32[16,128]{1,0:T(8,128)} %scale_ref.5) | copy-start | bytes 24580
  53.7 12.8 %all-to-all-start.2 = ((f32[32,4,128]{2,1,0:T(4,128)}), f32[32,4,128]{2,1,0:T(4,128)S(1)}, u32[]{:S(2)}, u32[]{:S(2)}) async-start(f32[32,4,128]{2,1,0:T(4,128)} %bitcast.5), calls=%async_computation.2 | async-start | bytes 131072 | tf_op jit(solution)/shard_map/all_to_all | solution.py:555
  59.6 1.2 %copy-start.3 = (f32[5,16]{1,0:T(8,128)S(1)}, f32[5,16]{1,0:T(8,128)}, u32[]{:S(2)}) copy-start(f32[5,16]{1,0:T(8,128)} %taps_ref.1) | copy-start | bytes 964
